TPU v7x, 32 devices: a whole 2x2x4 slice. The times are simulated.
32 devices in a mesh: band: 4 (over z), roster: 8 (over y, x, core).
Axes of the slice: x: 2, y: 2, z: 4, core: 2. Of those that a mesh axis runs over, the one named last changes fastest.
Arguments:
- tiles: bfloat16 [4, 8, 6, 256, 256], P('band', 'roster'), as said below
- tile_slots: int32 [4, 8, 6], P('band', 'roster'), may hold values from 0 to 5, each once within a row
- tile_count: int32 [4, 8], P('band', 'roster'), may hold values from 1 to 6, as said below
- costs: float32 [6144, 128], P('roster'), may hold values from 1000 to 10000
- primal_start: float32 [6144, 128], P('roster'), may hold values from 0 to 1
- dual_start: float32 [2048, 128], P('band'), may hold values from 0.5 to 4
Outputs:
- primal: float32 [6144, 128], P('roster')
- dual: float32 [2048, 128], P('band')
Inputs may be any that keep to these rules, and one draw needn't show every extreme that they name: `tile_slots`: each device's slots list every tile position once; slot s is in use where s < tile_count. `tile_count`: some device uses all 6 slots. `tiles`: entries are zero or positive.
All inputs are finite; a program needn't handle non-finite values.
Results may differ from a plain program's by a relative error of at most 0.0003.
Values sent between devices are 32-bit elements; how exact they have to be, the bound alone decides.
A program may use at most 64 MiB of HBM per device.

v0:
```python
import jax
import jax.numpy as jnp
from jax import lax
from jax.sharding import PartitionSpec as P

ROUNDS = 3
ITERS = 4
HIGH = lax.Precision.HIGHEST
eps = 1e-06


def shards(tiles, tile_slots, tile_count, costs, primal_start, dual_start):
    tile_block = tiles[0, 0]
    slots = tile_slots[0, 0]
    count = tile_count[0, 0]
    tile = tile_block.shape[1]
    rows = dual_start.shape[0]
    cols = costs.shape[0]
    row_tiles = rows // tile
    col_tiles = cols // tile
    row_index = slots // col_tiles
    col_index = slots % col_tiles
    active = (jnp.arange(slots.shape[0], dtype=jnp.int32) < count).astype(jnp.float32)
    row_hot = (row_index[None, :] == jnp.arange(row_tiles, dtype=jnp.int32)[:, None]).astype(
        jnp.float32
    )
    col_hot = (col_index[None, :] == jnp.arange(col_tiles, dtype=jnp.int32)[:, None]).astype(
        jnp.float32
    )

    def scale_tiles(row_scale, col_scale):
        row_part = row_scale.reshape(row_tiles, tile)[row_index]
        col_part = col_scale.reshape(col_tiles, tile)[col_index]
        return (
            tile_block.astype(jnp.float32)
            * row_part[:, :, None]
            * col_part[:, None, :]
            * active[:, None, None]
        )

    row_scale = jnp.ones((rows,), jnp.float32)
    col_scale = jnp.ones((cols,), jnp.float32)
    for turn in range(ROUNDS):
        magnitude = jnp.abs(scale_tiles(row_scale, col_scale))
        slot_rows = jnp.max(magnitude, axis=2)
        slot_cols = jnp.max(magnitude, axis=1)
        row_peak = jnp.max(row_hot[:, :, None] * slot_rows[None], axis=1).reshape(-1)
        col_peak = jnp.max(col_hot[:, :, None] * slot_cols[None], axis=1).reshape(-1)
        row_peak = lax.pmax(row_peak, "roster")
        col_peak = lax.pmax(col_peak, "band")
        row_scale = row_scale / jnp.sqrt(row_peak + eps)
        col_scale = col_scale / jnp.sqrt(col_peak + eps)
    scaled = scale_tiles(row_scale, col_scale)
    squares = lax.psum(jnp.sum(scaled * scaled), ("band", "roster"))
    eta = 0.9 / jnp.sqrt(squares + eps)
    scen = costs.shape[1]
    col_full = col_scale[:, None]
    row_full = row_scale[:, None]
    cost_t = costs * col_full
    upper = 1.0 / col_full
    primal = primal_start / col_full
    dual = dual_start / row_full
    for step in range(ITERS):
        dual_slots = dual.reshape(row_tiles, tile, scen)[row_index]
        back_terms = jnp.einsum("sij,sik->sjk", scaled, dual_slots, precision=HIGH)
        g_local = jnp.einsum("cs,sjk->cjk", col_hot, back_terms, precision=HIGH).reshape(cols, scen)
        g_whole = lax.psum(g_local, "band")
        primal_next = jnp.clip(primal - eta * (cost_t - g_whole), 0.0, upper)
        extrapolated = 2.0 * primal_next - primal
        primal_slots = extrapolated.reshape(col_tiles, tile, scen)[col_index]
        fore_terms = jnp.einsum("sij,sjk->sik", scaled, primal_slots, precision=HIGH)
        h_local = jnp.einsum("rs,sik->rik", row_hot, fore_terms, precision=HIGH).reshape(rows, scen)
        share = rows // lax.axis_size("roster")
        begin = lax.axis_index("roster") * share
        h_share = lax.psum_scatter(h_local, "roster", scatter_dimension=0, tiled=True)
        own_dual = lax.dynamic_slice_in_dim(dual, begin, share, 0)
        own_rows = lax.dynamic_slice_in_dim(row_full, begin, share, 0)
        dual_share = own_dual + eta * (own_rows - h_share)
        dual = lax.all_gather(dual_share, "roster", axis=0, tiled=True)
        primal = primal_next
    return (primal, dual)


def solution(mesh):
    placed = (
        P("band", "roster", None, None, None),
        P("band", "roster", None),
        P("band", "roster"),
        P("roster", None),
        P("roster", None),
        P("band", None),
    )
    return jax.shard_map(
        shards,
        mesh=mesh,
        in_specs=placed,
        out_specs=(P("roster", None), P("band", None)),
        check_vma=False,
    )
```

profile of v0, /device:TPU:0, one launch (start us, length us, event | category | flops | bytes accessed | tf_op | source)
XLA Modules:
  0.0 466.0 jit_solution(17935510203944272796)
XLA Ops:
  10.5 1.8 fusion.3
  12.4 15.1 %pmax.43 = f32[512]{0:T(512)S(1)} all-reduce(f32[512]{0:T(512)S(1)} %bitcast.135), channel_id=1, replica_groups=mesh['band'=4,'roster'=8] {'roster'}, use_global_device_ids=true, to_apply=%region_5.6 | all-reduce | flops 512 | bytes 4096 | tf_op jit(solution)/shard_map/pmax | solution.py:49
  27.7 12.0 %pmax.42 = f32[768]{0:T(1024)S(1)} all-reduce(f32[768]{0:T(1024)S(1)} %reshape.279), channel_id=1, replica_groups=mesh['band'=4,'roster'=8] {'band'}, use_global_device_ids=true, to_apply=%region_2.3 | all-reduce | flops 768 | bytes 6144 | tf_op jit(solution)/shard_map/pmax | solution.py:50
  41.6 8.4 %pmax.44 = f32[768]{0:T(1024)S(1)} all-reduce(f32[768]{0:T(1024)S(1)} %reshape.283), channel_id=1, replica_groups=mesh['band'=4,'roster'=8] {'band'}, use_global_device_ids=true, to_apply=%region_8.9 | all-reduce | flops 768 | bytes 6144 | tf_op jit(solution)/shard_map/pmax | solution.py:50
  50.0 11.8 %pmax.45 = f32[512]{0:T(512)S(1)} all-reduce(f32[512]{0:T(512)S(1)} %bitcast.136), channel_id=1, replica_groups=mesh['band'=4,'roster'=8] {'roster'}, use_global_device_ids=true, to_apply=%region_11.12 | all-reduce | flops 512 | bytes 4096 | tf_op jit(solution)/shard_map/pmax | solution.py:49
  63.8 10.4 %pmax.46 = f32[768]{0:T(1024)S(1)} all-reduce(f32[768]{0:T(1024)S(1)} %reshape.287), channel_id=1, replica_groups=mesh['band'=4,'roster'=8] {'band'}, use_global_device_ids=true, to_apply=%region_14.15 | all-reduce | flops 768 | bytes 6144 | tf_op jit(solution)/shard_map/pmax | solution.py:50
  74.2 11.8 %pmax.47 = f32[512]{0:T(512)S(1)} all-reduce(f32[512]{0:T(512)S(1)} %bitcast.137), channel_id=1, replica_groups=mesh['band'=4,'roster'=8] {'roster'}, use_global_device_ids=true, to_apply=%region_17.18 | all-reduce | flops 512 | bytes 4096 | tf_op jit(solution)/shard_map/pmax | solution.py:49
  87.9 2.9 fusion.31
  93.9 37.9 %psum.35 = f32[]{:T(128)} all-reduce(f32[]{:T(128)} %fusion.34), channel_id=1, replica_groups=mesh['band'=4,'roster'=8] {'band','roster'}, use_global_device_ids=true, to_apply=%region_19.20 | all-reduce | flops 1 | bytes 8 | tf_op jit(solution)/shard_map/psum | solution.py:54
  138.2 33.9 %reduce-scatter.5.cloned.1.call-done = f32[64,128]{1,0:T(8,128)} async-done(((f32[512,128]{1,0:T(8,128)}), f32[64,128]{1,0:T(8,128)}) %reduce-scatter.5.cloned.1.call-update) | async-done | bytes 32784 | tf_op jit(solution)/shard_map/reduce_scatter | solution.py:75
  172.8 9.7 %all_gather.12 = f32[512,128]{1,0:T(8,128)S(1)} all-gather(f32[64,128]{1,0:T(8,128)S(1)} %multiply_add_fusion.3), channel_id=1, replica_groups=mesh['band'=4,'roster'=8] {'roster'}, dimensions={0}, use_global_device_ids=true | all-gather | bytes 294912 | tf_op jit(solution)/shard_map/all_gather | solution.py:79
  183.2 3.0 fusion.27
  188.0 37.0 %all-reduce.7.cloned.1.call-done = f32[768,128]{1,0:T(8,128)} async-done(((f32[768,128]{1,0:T(8,128)}), f32[768,128]{1,0:T(8,128)}) %all-reduce.7.cloned.1.call-update) | async-done | bytes 393232 | tf_op jit(solution)/shard_map/psum | solution.py:67
  230.4 33.5 %reduce-scatter.7.cloned.1.call-done = f32[64,128]{1,0:T(8,128)} async-done(((f32[512,128]{1,0:T(8,128)}), f32[64,128]{1,0:T(8,128)}) %reduce-scatter.7.cloned.1.call-update) | async-done | bytes 32784 | tf_op jit(solution)/shard_map/reduce_scatter | solution.py:75
  264.8 9.4 %all_gather.13 = f32[512,128]{1,0:T(8,128)S(1)} all-gather(f32[64,128]{1,0:T(8,128)S(1)} %multiply_add_fusion.2), channel_id=1, replica_groups=mesh['band'=4,'roster'=8] {'roster'}, dimensions={0}, use_global_device_ids=true | all-gather | bytes 294912 | tf_op jit(solution)/shard_map/all_gather | solution.py:79
  274.8 3.0 fusion.23
  279.6 37.1 %all-reduce.9.cloned.1.call-done = f32[768,128]{1,0:T(8,128)} async-done(((f32[768,128]{1,0:T(8,128)}), f32[768,128]{1,0:T(8,128)}) %all-reduce.9.cloned.1.call-update) | async-done | bytes 393232 | tf_op jit(solution)/shard_map/psum | solution.py:67
  322.1 33.5 %reduce-scatter.9.cloned.1.call-done = f32[64,128]{1,0:T(8,128)} async-done(((f32[512,128]{1,0:T(8,128)}), f32[64,128]{1,0:T(8,128)}) %reduce-scatter.9.cloned.1.call-update) | async-done | bytes 32784 | tf_op jit(solution)/shard_map/reduce_scatter | solution.py:75
  356.5 9.5 %all_gather.14 = f32[512,128]{1,0:T(8,128)S(1)} all-gather(f32[64,128]{1,0:T(8,128)S(1)} %multiply_add_fusion.1), channel_id=1, replica_groups=mesh['band'=4,'roster'=8] {'roster'}, dimensions={0}, use_global_device_ids=true | all-gather | bytes 294912 | tf_op jit(solution)/shard_map/all_gather | solution.py:79
  366.6 3.0 fusion.19
  371.4 37.1 %all-reduce.11.cloned.1.call-done = f32[768,128]{1,0:T(8,128)} async-done(((f32[768,128]{1,0:T(8,128)}), f32[768,128]{1,0:T(8,128)}) %all-reduce.11.cloned.1.call-update) | async-done | bytes 393232 | tf_op jit(solution)/shard_map/psum | solution.py:67
  408.4 2.0 multiply_subtract_fusion
  414.6 33.6 %reduce-scatter.11.cloned.1.call-done = f32[64,128]{1,0:T(8,128)} async-done(((f32[512,128]{1,0:T(8,128)}), f32[64,128]{1,0:T(8,128)}) %reduce-scatter.11.cloned.1.call-update) | async-done | bytes 32784 | tf_op jit(solution)/shard_map/reduce_scatter | solution.py:75
  449.0 9.2 %all_gather.15 = f32[512,128]{1,0:T(8,128)S(1)} all-gather(f32[64,128]{1,0:T(8,128)S(1)} %multiply_add_fusion), channel_id=1, replica_groups=mesh['band'=4,'roster'=8] {'roster'}, dimensions={0}, use_global_device_ids=true | all-gather | bytes 294912 | tf_op jit(solution)/shard_map/all_gather | solution.py:79
  (107 shorter events, 43.4 us)
Async XLA Ops:
  7.2 33.6 %copy-start = (bf16[1,1,6,256,256]{4,3,2,1,0:T(8,128)(2,1)S(1)}, bf16[1,1,6,256,256]{4,3,2,1,0:T(8,128)(2,1)}, u32[]{:S(2)}) copy-start(bf16[1,1,6,256,256]{4,3,2,1,0:T(8,128)(2,1)} %param.6) | copy-start | bytes 2359300
  7.2 125.4 %all-reduce.5.cloned.1.call-start = ((), (), s32[]{:S(2)}) async-start(), calls=%async_computation.4 | async-start | bytes 786432 | tf_op jit(solution)/shard_map/psum | solution.py:67
  41.4 45.7 %copy-start.3 = (f32[512,128]{1,0:T(8,128)S(1)}, f32[512,128]{1,0:T(8,128)}, u32[]{:S(2)}) copy-start(f32[512,128]{1,0:T(8,128)} %param.11) | copy-start | bytes 786436
  92.7 39.9 %copy-start.1 = (f32[768,128]{1,0:T(8,128)S(1)}, f32[768,128]{1,0:T(8,128)}, u32[]{:S(2)}) copy-start(f32[768,128]{1,0:T(8,128)} %param.9) | copy-start | bytes 1179652
  92.7 39.9 %copy-start.2 = (f32[768,128]{1,0:T(8,128)S(1)}, f32[768,128]{1,0:T(8,128)}, u32[]{:S(2)}) copy-start(f32[768,128]{1,0:T(8,128)} %param.10) | copy-start | bytes 1179652
  92.7 79.3 %reduce-scatter.5.cloned.1.call-start = ((), (), s32[]{:S(2)}) async-start(), calls=%async_computation.5 | async-start | bytes 294912 | tf_op jit(solution)/shard_map/reduce_scatter | solution.py:75
  138.0 87.0 %all-reduce.7.cloned.1.call-start = ((), (), s32[]{:S(2)}) async-start(), calls=%async_computation.6 | async-start | bytes 786432 | tf_op jit(solution)/shard_map/psum | solution.py:67
  187.9 76.1 %reduce-scatter.7.cloned.1.call-start = ((), (), s32[]{:S(2)}) async-start(), calls=%async_computation.7 | async-start | bytes 294912 | tf_op jit(solution)/shard_map/reduce_scatter | solution.py:75
  230.4 86.3 %all-reduce.9.cloned.1.call-start = ((), (), s32[]{:S(2)}) async-start(), calls=%async_computation.8 | async-start | bytes 786432 | tf_op jit(solution)/shard_map/psum | solution.py:67
  279.6 76.1 %reduce-scatter.9.cloned.1.call-start = ((), (), s32[]{:S(2)}) async-start(), calls=%async_computation.9 | async-start | bytes 294912 | tf_op jit(solution)/shard_map/reduce_scatter | solution.py:75
  322.1 86.4 %all-reduce.11.cloned.1.call-start = ((), (), s32[]{:S(2)}) async-start(), calls=%async_computation.10 | async-start | bytes 786432 | tf_op jit(solution)/shard_map/psum | solution.py:67
  371.3 76.8 %reduce-scatter.11.cloned.1.call-start = ((), (), s32[]{:S(2)}) async-start(), calls=%async_computation.11 | async-start | bytes 294912 | tf_op jit(solution)/shard_map/reduce_scatter | solution.py:75
Sparse Core Ops, SparseCore 0:
  92.8 33.2 all-reduce.4
  138.1 33.8 reduce-scatter.4
  188.0 36.9 all-reduce.6
  230.5 33.4 reduce-scatter.6
  279.7 36.9 all-reduce.8
  322.2 33.4 reduce-scatter.8
  371.5 36.9 all-reduce.10
  414.7 33.4 reduce-scatter.10
where the time goes:
time: 475 us; the launch traced here: 466 us
  waiting for transfers between devices  246 us (52%)
  blocking collectives  145 us (31%)
  matrix products  26.8 us (6%)
  local copies, waits for them, and re-layouts  16.3 us (3%)
  between operations  16.1 us (3%)
  other arithmetic  15.4 us (3%)
    reduce_scatter x4, waiting for transfers between devices, shards(): lax.psum_scatter(h_local, 'roster', scatter_dimension=0, tiled=True)  135 us
    psum x4, waiting for transfers between devices, shards(): g_whole = lax.psum(g_local, 'band')  111 us
    pmax x3, blocking collectives, shards(): row_peak = lax.pmax(row_peak, 'roster')  38.7 us
    psum x1, blocking collectives, shards(): squares = lax.psum(jnp.sum(scaled * scaled), ('band', 'roster'))  37.9 us
    all_gather x4, blocking collectives, shards(): dual = lax.all_gather(dual_share, 'roster', axis=0, tiled=True)  37.8 us
    pmax x3, blocking collectives, shards(): col_peak = lax.pmax(col_peak, 'band')  30.7 us
    dot_general x4, matrix products, shards(): back_terms = jnp.einsum('sij,sik->sjk', scaled, dual_slots, precision=HIGH)  11.8 us
  transfers between devices with their start and end apart: 8, of which 7 were waited for; matrix products, arithmetic and copies ran while one was open for 0% of the time, Pallas kernels for 0%

commit v1 on v0

--- a/solution.py
+++ b/solution.py
@@ -76,7 +76,16 @@
         own_dual = lax.dynamic_slice_in_dim(dual, begin, share, 0)
         own_rows = lax.dynamic_slice_in_dim(row_full, begin, share, 0)
         dual_share = own_dual + eta * (own_rows - h_share)
-        dual = lax.all_gather(dual_share, "roster", axis=0, tiled=True)
+        ring = [dual_share]
+        for hop in range(7):
+            ring.append(
+                lax.ppermute(ring[-1], "roster", [(dev, (dev + 1) % 8) for dev in range(8)])
+            )
+        dual = jnp.roll(
+            jnp.concatenate(ring[::-1], axis=0),
+            (lax.axis_index("roster") + 1) * ring[0].shape[0],
+            axis=0,
+        )
         primal = primal_next
     return (primal, dual)
 

time: 475 us -> 558 us (1.17)
  waiting for transfers between devices: 246 us -> 364 us
  blocking collectives: 145 us -> 107 us
    ppermute x0 -> x28, waiting for transfers between devices: none -> 119 us  [shards(): lax.ppermute(ring[-1], 'roster', [(dev, (dev + 1) % 8) for dev in range(8)])]
    all_gather x4 -> x0, blocking collectives: 37.8 us -> none  [shards(): dual = lax.all_gather(dual_share, 'roster', axis=0, tiled=True)]
  transfers between devices with their start and end apart: 8 -> 36, of which waited for: 7 -> 35; matrix products, arithmetic and copies ran while one was open for 0% -> 0% of each run, Pallas kernels for 0% -> 0%
where the time goes in v1:
time: 558 us; the launch traced here: 549 us
  waiting for transfers between devices  364 us (65%)
  blocking collectives  107 us (19%)
  matrix products  26.8 us (5%)
  other arithmetic  16.8 us (3%)
  between operations  16.4 us (3%)
  local copies, waits for them, and re-layouts  15.7 us (3%)
    reduce_scatter x4, waiting for transfers between devices, shards(): lax.psum_scatter(h_local, 'roster', scatter_dimension=0, tiled=True)  134 us
    ppermute x28, waiting for transfers between devices, shards(): lax.ppermute(ring[-1], 'roster', [(dev, (dev + 1) % 8) for dev in range(8)])  119 us
    psum x4, waiting for transfers between devices, shards(): g_whole = lax.psum(g_local, 'band')  111 us
    pmax x3, blocking collectives, shards(): row_peak = lax.pmax(row_peak, 'roster')  38.7 us
    psum x1, blocking collectives, shards(): squares = lax.psum(jnp.sum(scaled * scaled), ('band', 'roster'))  38 us
    pmax x3, blocking collectives, shards(): col_peak = lax.pmax(col_peak, 'band')  30.7 us
    dot_general x4, matrix products, shards(): back_terms = jnp.einsum('sij,sik->sjk', scaled, dual_slots, precision=HIGH)  11.8 us
  transfers between devices with their start and end apart: 36, of which 35 were waited for; matrix products, arithmetic and copies ran while one was open for 0% of the time, Pallas kernels for 0%

profile of v1, /device:TPU:0, one launch (start us, length us, event | category | flops | bytes accessed | tf_op | source)
XLA Modules:
  0.0 548.8 jit_solution(10455361344656175418)
XLA Ops:
  12.4 15.1 %pmax.43 = f32[512]{0:T(512)S(1)} all-reduce(f32[512]{0:T(512)S(1)} %bitcast.135), channel_id=1, replica_groups=mesh['band'=4,'roster'=8] {'roster'}, use_global_device_ids=true, to_apply=%region_5.6 | all-reduce | flops 512 | bytes 4096 | tf_op jit(solution)/shard_map/pmax | solution.py:49
  27.7 12.0 %pmax.42 = f32[768]{0:T(1024)S(1)} all-reduce(f32[768]{0:T(1024)S(1)} %reshape.279), channel_id=1, replica_groups=mesh['band'=4,'roster'=8] {'band'}, use_global_device_ids=true, to_apply=%region_2.3 | all-reduce | flops 768 | bytes 6144 | tf_op jit(solution)/shard_map/pmax | solution.py:50
  41.6 8.4 %pmax.44 = f32[768]{0:T(1024)S(1)} all-reduce(f32[768]{0:T(1024)S(1)} %reshape.283), channel_id=1, replica_groups=mesh['band'=4,'roster'=8] {'band'}, use_global_device_ids=true, to_apply=%region_8.9 | all-reduce | flops 768 | bytes 6144 | tf_op jit(solution)/shard_map/pmax | solution.py:50
  50.0 11.8 %pmax.45 = f32[512]{0:T(512)S(1)} all-reduce(f32[512]{0:T(512)S(1)} %bitcast.136), channel_id=1, replica_groups=mesh['band'=4,'roster'=8] {'roster'}, use_global_device_ids=true, to_apply=%region_11.12 | all-reduce | flops 512 | bytes 4096 | tf_op jit(solution)/shard_map/pmax | solution.py:49
  63.8 10.4 %pmax.46 = f32[768]{0:T(1024)S(1)} all-reduce(f32[768]{0:T(1024)S(1)} %reshape.287), channel_id=1, replica_groups=mesh['band'=4,'roster'=8] {'band'}, use_global_device_ids=true, to_apply=%region_14.15 | all-reduce | flops 768 | bytes 6144 | tf_op jit(solution)/shard_map/pmax | solution.py:50
  74.2 11.8 %pmax.47 = f32[512]{0:T(512)S(1)} all-reduce(f32[512]{0:T(512)S(1)} %bitcast.137), channel_id=1, replica_groups=mesh['band'=4,'roster'=8] {'roster'}, use_global_device_ids=true, to_apply=%region_17.18 | all-reduce | flops 512 | bytes 4096 | tf_op jit(solution)/shard_map/pmax | solution.py:49
  93.9 38.0 %psum.35 = f32[]{:T(128)} all-reduce(f32[]{:T(128)} %fusion.34), channel_id=1, replica_groups=mesh['band'=4,'roster'=8] {'band','roster'}, use_global_device_ids=true, to_apply=%region_19.20 | all-reduce | flops 1 | bytes 8 | tf_op jit(solution)/shard_map/psum | solution.py:54
  138.2 33.8 %reduce-scatter.5.cloned.1.call-done = f32[64,128]{1,0:T(8,128)} async-done(((f32[512,128]{1,0:T(8,128)}), f32[64,128]{1,0:T(8,128)}) %reduce-scatter.5.cloned.1.call-update) | async-done | bytes 32784 | tf_op jit(solution)/shard_map/reduce_scatter | solution.py:75
  177.5 4.2 collective-permute-done.1
  181.8 4.2 collective-permute-done.2
  190.3 4.2 collective-permute-done.4
  194.5 4.2 collective-permute-done.5
  208.6 37.1 %all-reduce.7.cloned.1.call-done = f32[768,128]{1,0:T(8,128)} async-done(((f32[768,128]{1,0:T(8,128)}), f32[768,128]{1,0:T(8,128)}) %all-reduce.7.cloned.1.call-update) | async-done | bytes 393232 | tf_op jit(solution)/shard_map/psum | solution.py:67
  251.2 33.5 %reduce-scatter.7.cloned.1.call-done = f32[64,128]{1,0:T(8,128)} async-done(((f32[512,128]{1,0:T(8,128)}), f32[64,128]{1,0:T(8,128)}) %reduce-scatter.7.cloned.1.call-update) | async-done | bytes 32784 | tf_op jit(solution)/shard_map/reduce_scatter | solution.py:75
  289.8 4.2 collective-permute-done.8
  294.0 4.2 collective-permute-done.9
  306.8 4.2 collective-permute-done.12
  321.1 37.0 %all-reduce.9.cloned.1.call-done = f32[768,128]{1,0:T(8,128)} async-done(((f32[768,128]{1,0:T(8,128)}), f32[768,128]{1,0:T(8,128)}) %all-reduce.9.cloned.1.call-update) | async-done | bytes 393232 | tf_op jit(solution)/shard_map/psum | solution.py:67
  363.6 33.5 %reduce-scatter.9.cloned.1.call-done = f32[64,128]{1,0:T(8,128)} async-done(((f32[512,128]{1,0:T(8,128)}), f32[64,128]{1,0:T(8,128)}) %reduce-scatter.9.cloned.1.call-update) | async-done | bytes 32784 | tf_op jit(solution)/shard_map/reduce_scatter | solution.py:75
  406.4 4.2 collective-permute-done.16
  419.1 4.2 collective-permute-done.19
  433.5 37.0 %all-reduce.11.cloned.1.call-done = f32[768,128]{1,0:T(8,128)} async-done(((f32[768,128]{1,0:T(8,128)}), f32[768,128]{1,0:T(8,128)}) %all-reduce.11.cloned.1.call-update) | async-done | bytes 393232 | tf_op jit(solution)/shard_map/psum | solution.py:67
  476.7 33.6 %reduce-scatter.11.cloned.1.call-done = f32[64,128]{1,0:T(8,128)} async-done(((f32[512,128]{1,0:T(8,128)}), f32[64,128]{1,0:T(8,128)}) %reduce-scatter.11.cloned.1.call-update) | async-done | bytes 32784 | tf_op jit(solution)/shard_map/reduce_scatter | solution.py:75
  515.4 4.2 collective-permute-done.22
  (194 shorter events, 137.0 us)
Async XLA Ops:
  7.2 125.4 %all-reduce.5.cloned.1.call-start = ((), (), s32[]{:S(2)}) async-start(), calls=%async_computation.4 | async-start | bytes 786432 | tf_op jit(solution)/shard_map/psum | solution.py:67
  92.7 79.3 %reduce-scatter.5.cloned.1.call-start = ((), (), s32[]{:S(2)}) async-start(), calls=%async_computation.5 | async-start | bytes 294912 | tf_op jit(solution)/shard_map/reduce_scatter | solution.py:75
  138.0 107.7 %all-reduce.7.cloned.1.call-start = ((), (), s32[]{:S(2)}) async-start(), calls=%async_computation.6 | async-start | bytes 786432 | tf_op jit(solution)/shard_map/psum | solution.py:67
  172.8 4.7 collective-permute-start
  177.5 4.2 collective-permute-start.1
  181.8 4.2 collective-permute-start.2
  186.0 4.2 collective-permute-start.3
  194.5 4.2 collective-permute-start.5
  208.6 76.1 %reduce-scatter.7.cloned.1.call-start = ((), (), s32[]{:S(2)}) async-start(), calls=%async_computation.7 | async-start | bytes 294912 | tf_op jit(solution)/shard_map/reduce_scatter | solution.py:75
  251.1 107.0 %all-reduce.9.cloned.1.call-start = ((), (), s32[]{:S(2)}) async-start(), calls=%async_computation.8 | async-start | bytes 786432 | tf_op jit(solution)/shard_map/psum | solution.py:67
  285.5 4.3 collective-permute-start.7
  294.0 4.2 collective-permute-start.9
  306.8 4.2 collective-permute-start.12
  311.0 4.4 collective-permute-start.13
  321.0 76.1 %reduce-scatter.9.cloned.1.call-start = ((), (), s32[]{:S(2)}) async-start(), calls=%async_computation.9 | async-start | bytes 294912 | tf_op jit(solution)/shard_map/reduce_scatter | solution.py:75
  363.5 107.0 %all-reduce.11.cloned.1.call-start = ((), (), s32[]{:S(2)}) async-start(), calls=%async_computation.10 | async-start | bytes 786432 | tf_op jit(solution)/shard_map/psum | solution.py:67
  397.9 4.3 collective-permute-start.14
  406.4 4.2 collective-permute-start.16
  419.1 4.2 collective-permute-start.19
  423.4 4.4 collective-permute-start.20
  433.4 76.8 %reduce-scatter.11.cloned.1.call-start = ((), (), s32[]{:S(2)}) async-start(), calls=%async_computation.11 | async-start | bytes 294912 | tf_op jit(solution)/shard_map/reduce_scatter | solution.py:75
  511.1 4.3 collective-permute-start.21
  515.4 4.2 collective-permute-start.22
  528.1 4.2 collective-permute-start.25
  (16 other events, 210.1 us)
Sparse Core Ops, SparseCore 0:
  92.8 33.2 all-reduce.4
  138.2 33.7 reduce-scatter.4
  208.7 36.9 all-reduce.6
  251.2 33.4 reduce-scatter.6
  321.1 36.9 all-reduce.8
  363.6 33.4 reduce-scatter.8
  433.6 36.9 all-reduce.10
  476.8 33.4 reduce-scatter.10
